TPU v7x, 32 devices: a whole 2x2x4 slice. The times are simulated.
32 devices in a mesh: depth: 8 (over z, y), space: 4 (over x, core).
Axes of the slice: x: 2, y: 2, z: 4, core: 2. Of those that a mesh axis runs over, the one named last changes fastest.
Arguments:
- coarse_states: float32 [8, 32, 128, 128], P('depth', 'space'), may hold values from -6 to 6
- first_kernels: bfloat16 [32, 9, 128, 128], P('depth'), may hold values from -0.1875 to 0.1875
- second_kernels: bfloat16 [32, 9, 128, 128], P('depth'), may hold values from -0.1875 to 0.1875
- coarse_channel_gain: float32 [8, 128], replicated, may hold values from 0 to 1, as said below
Outputs:
- states: float32 [32, 32, 128, 128], P('depth', 'space')
- relaxed: float32 [8, 32, 128, 128], P('depth', 'space')
Inputs may be any that keep to these rules, and one draw needn't show every extreme that they name: `coarse_channel_gain`: each entry is positive and at most 1.
All inputs are finite; a program needn't handle non-finite values.
Results may differ from a plain program's by a relative error of at most 0.01.
Values may be sent and summed in bfloat16 or wider, within the bound.
A program may use at most 128 MiB of HBM per device.

v0:
```python
import functools

import jax
import jax.numpy as jnp
from jax import lax
from jax.experimental import pallas as pl
from jax.experimental.pallas import tpu as pltpu
from jax.sharding import PartitionSpec as P

MESH = pl.DeviceIdType.MESH
F32 = jnp.float32
BF16 = jnp.bfloat16


def conv_pairs(row, starts, taps):
    lhs = jnp.concatenate(
        [jnp.concatenate([row(s + i) for s in starts], axis=0) for i in range(4)], axis=1
    )
    count = lhs.shape[0]
    cols = count // len(starts)
    parts = []
    for b in range(3):
        top, mid, low = (taps(3 * a + b) for a in range(3))
        none = jnp.zeros_like(top)
        weight = jnp.concatenate(
            [
                jnp.concatenate([top, none], axis=1),
                jnp.concatenate([mid, top], axis=1),
                jnp.concatenate([low, mid], axis=1),
                jnp.concatenate([none, low], axis=1),
            ],
            axis=0,
        )
        parts.append(jnp.dot(lhs, weight, preferred_element_type=F32))
    column = lax.broadcasted_iota(jnp.int32, parts[0].shape, 0) % cols
    left = jnp.where(column == 0, 0.0, pltpu.roll(parts[0], 1, 0))
    right = jnp.where(column == cols - 1, 0.0, pltpu.roll(parts[2], count - 1, 0))
    return parts[1] + left + right


def cycle_kernel(
    depths,
    spaces,
    start_ref,
    first_ref,
    second_ref,
    gain_ref,
    states_ref,
    relaxed_ref,
    xbuf,
    hbuf,
    sbuf,
    ybuf,
    cbuf,
    qsend,
    qrecv,
    tsend,
    trecv,
    fsend,
    frecv,
    halo_send,
    halo_recv,
    y_send,
    y_recv,
    scan_send,
    scan_recv,
    out_sem,
    relaxed_sem,
):
    layers = first_ref.shape[0]
    rows, cols, chans = start_ref.shape
    half = rows // 2
    d = lax.axis_index("depth")
    s = lax.axis_index("space")
    odd = d % 2
    partner = d + 1 - 2 * odd

    barrier = pltpu.get_barrier_semaphore()

    meets = [
        (s > 0, (d, s - 1)),
        (s < spaces - 1, (d, s + 1)),
        (d > 0, (d - 1, s)),
        (d < depths - 1, (d + 1, s)),
        (d > 1, (d - 2, s)),
        (d < depths - 2, (d + 2, s)),
    ]
    def greet(there, device):
        @pl.when(there)
        def _():
            pl.semaphore_signal(barrier, inc=1, device_id=device, device_id_type=MESH)

    for there, device in meets:
        greet(there, device)
    pl.semaphore_wait(barrier, sum(there.astype(jnp.int32) for there, _ in meets))

    def halo_up(slot):
        return pltpu.make_async_remote_copy(
            src_ref=xbuf.at[slot, pl.ds(2, 2)],
            dst_ref=xbuf.at[slot, pl.ds(rows + 2, 2)],
            send_sem=halo_send.at[slot, 0],
            recv_sem=halo_recv.at[slot, 0],
            device_id=(d, s - 1),
            device_id_type=MESH,
        )

    def halo_down(slot):
        return pltpu.make_async_remote_copy(
            src_ref=xbuf.at[slot, pl.ds(rows, 2)],
            dst_ref=xbuf.at[slot, pl.ds(0, 2)],
            send_sem=halo_send.at[slot, 1],
            recv_sem=halo_recv.at[slot, 1],
            device_id=(d, s + 1),
            device_id_type=MESH,
        )

    def halo_start(slot):
        @pl.when(s > 0)
        def _():
            halo_up(slot).start()

        @pl.when(s < spaces - 1)
        def _():
            halo_down(slot).start()

    def halo_wait(slot):
        @pl.when(s < spaces - 1)
        def _():
            halo_up(slot).wait_recv()
            halo_down(slot).wait_send()

        @pl.when(s > 0)
        def _():
            halo_down(slot).wait_recv()
            halo_up(slot).wait_send()

    def layer(index, slot, src, dst, keep):
        def hidden_rows(starts):
            out = conv_pairs(lambda r: xbuf[slot, r], starts, lambda k: first_ref[index, k])
            out = jnp.tanh(out).astype(BF16)
            for n, r in enumerate(starts):
                hbuf[r] = out[n * cols : (n + 1) * cols, :chans]
                hbuf[r + 1] = out[n * cols : (n + 1) * cols, chans:]

        def state_rows(starts):
            out = conv_pairs(lambda r: hbuf[r], starts, lambda k: second_ref[index, k])
            out = 0.5 * jnp.tanh(out)
            for n, r in enumerate(starts):
                for i in range(2):
                    new = sbuf[src, r + i] + out[n * cols : (n + 1) * cols, i * chans : (i + 1) * chans]
                    sbuf[dst, r + i] = new
                    xbuf[1 - slot, r + i + 2] = new.astype(BF16)

        hidden_rows(range(2, rows, 2))
        state_rows(range(2, rows - 2, 2))
        halo_wait(slot)
        hidden_rows((0, rows))

        @pl.when(s == 0)
        def _():
            hbuf[0] = jnp.zeros_like(hbuf[0])

        @pl.when(s == spaces - 1)
        def _():
            hbuf[rows + 1] = jnp.zeros_like(hbuf[rows + 1])

        state_rows((0, rows - 2))

        @pl.when(keep)
        def _():
            halo_start(1 - slot)

    @pl.when(s == 0)
    def _():
        for slot in range(2):
            xbuf[slot, pl.ds(0, 2)] = jnp.zeros((2, cols, chans), BF16)

    @pl.when(s == spaces - 1)
    def _():
        for slot in range(2):
            xbuf[slot, pl.ds(rows + 2, 2)] = jnp.zeros((2, cols, chans), BF16)

    def begin(slot, source):
        xbuf[slot, pl.ds(2, rows)] = sbuf[source].astype(BF16)
        halo_start(slot)

    sbuf[layers] = start_ref[...]
    begin(0, layers)

    def first_sweep(i, carry):
        layer(i, i % 2, layers, layers, i < layers - 1)
        return carry

    lax.fori_loop(0, layers, first_sweep, 0)

    y_copy = pltpu.make_async_remote_copy(
        src_ref=ybuf,
        dst_ref=cbuf,
        send_sem=y_send,
        recv_sem=y_recv,
        device_id=(d + 1, s),
        device_id_type=MESH,
    )
    ybuf[...] = sbuf[layers].astype(BF16)

    @pl.when(d < depths - 1)
    def _():
        y_copy.start()

    @pl.when(d == 0)
    def _():
        sbuf[0] = start_ref[...]

    @pl.when(d > 0)
    def _():
        y_copy.wait_recv()
        sbuf[0] = cbuf[...].astype(F32)

    begin(layers % 2, 0)

    def second_sweep(i, carry):
        layer(i, (layers + i) % 2, layers * ((i + layers - 1) // layers), layers, i < layers - 1)
        return carry

    lax.fori_loop(0, layers, second_sweep, 0)

    relaxed_copy = pltpu.make_async_copy(sbuf.at[layers], relaxed_ref.at[0], relaxed_sem)
    relaxed_copy.start()

    def scan_copy(kind, r, src, dst, device):
        return pltpu.make_async_remote_copy(
            src_ref=src.at[r],
            dst_ref=dst.at[r],
            send_sem=scan_send.at[kind, r],
            recv_sem=scan_recv.at[kind, r],
            device_id=(device, s),
            device_id_type=MESH,
        )

    mine = odd * half
    theirs = half - mine
    for r in range(half):
        qsend[r] = (sbuf[layers, theirs + r] - ybuf[theirs + r].astype(F32)).astype(BF16)
        scan_copy(0, r, qsend, qrecv, partner).start()

    even = d - odd
    gain_odd = gain_ref[pl.ds((even + 1) % depths, 1), :]
    gain_next = gain_ref[pl.ds((even + 2) % depths, 1), :]

    @pl.when(d < 2)
    def _():
        trecv[...] = jnp.zeros_like(trecv)

    for r in range(half):
        own = sbuf[layers, mine + r] - ybuf[mine + r].astype(F32)
        scan_copy(0, r, qsend, qrecv, partner).wait_recv()
        other = qrecv[r].astype(F32)
        q_even = jnp.where(odd == 0, own, other)
        q_odd = jnp.where(odd == 0, other, own)

        @pl.when(d > 1)
        def _():
            scan_copy(1, r, tsend, trecv, d + 2).wait_recv()

        e_even = trecv[r].astype(F32)
        e_odd = gain_odd * e_even + q_even

        @pl.when(d < depths - 2)
        def _():
            tsend[r] = (gain_next * e_odd + q_odd).astype(BF16)
            scan_copy(1, r, tsend, trecv, d + 2).start()

        fsend[r] = jnp.where(odd == 0, e_odd, e_even).astype(BF16)
        scan_copy(2, r, fsend, frecv, partner).start()
        sbuf[0, mine + r] = sbuf[0, mine + r] + jnp.where(odd == 0, e_even, e_odd)

    for r in range(half):
        scan_copy(2, r, fsend, frecv, partner).wait_recv()
        sbuf[0, theirs + r] = sbuf[0, theirs + r] + frecv[r].astype(F32)

    begin((2 * layers) % 2, 0)

    def out_copy(i):
        return pltpu.make_async_copy(sbuf.at[i], states_ref.at[i], out_sem.at[i])

    out_copy(0).start()

    def third_sweep(i, carry):
        layer(i, i % 2, i, i + 1, i < layers - 2)
        out_copy(i + 1).start()
        return carry

    lax.fori_loop(0, layers - 1, third_sweep, 0)

    @pl.when(d < depths - 1)
    def _():
        y_copy.wait_send()

    for r in range(half):
        scan_copy(0, r, qsend, qrecv, partner).wait_send()
        scan_copy(2, r, fsend, frecv, partner).wait_send()

        @pl.when(d < depths - 2)
        def _():
            scan_copy(1, r, tsend, trecv, d + 2).wait_send()

    relaxed_copy.wait()
    for i in range(layers):
        out_copy(i).wait()


def shards(depths, spaces, coarse_states, first_kernels, second_kernels, coarse_channel_gain):
    layers, taps, chans, _ = first_kernels.shape
    _, rows, cols, _ = coarse_states.shape
    half = rows // 2
    vmem = pl.BlockSpec(memory_space=pltpu.VMEM)
    hbm = pl.BlockSpec(memory_space=pl.ANY)
    part = pltpu.VMEM((half, cols, chans), BF16)
    return pl.pallas_call(
        functools.partial(cycle_kernel, depths, spaces),
        out_shape=(
            jax.ShapeDtypeStruct((layers, rows, cols, chans), F32),
            jax.ShapeDtypeStruct((1, rows, cols, chans), F32),
        ),
        in_specs=[vmem] * 4,
        out_specs=(hbm, hbm),
        scratch_shapes=[
            pltpu.VMEM((2, rows + 4, cols, chans), BF16),
            pltpu.VMEM((rows + 2, cols, chans), BF16),
            pltpu.VMEM((layers + 1, rows, cols, chans), F32),
            pltpu.VMEM((rows, cols, chans), BF16),
            pltpu.VMEM((rows, cols, chans), BF16),
            part,
            part,
            part,
            part,
            part,
            part,
            pltpu.SemaphoreType.DMA((2, 2)),
            pltpu.SemaphoreType.DMA((2, 2)),
            pltpu.SemaphoreType.DMA,
            pltpu.SemaphoreType.DMA,
            pltpu.SemaphoreType.DMA((3, half)),
            pltpu.SemaphoreType.DMA((3, half)),
            pltpu.SemaphoreType.DMA((layers,)),
            pltpu.SemaphoreType.DMA,
        ],
        compiler_params=pltpu.CompilerParams(
            collective_id=0, has_side_effects=True, vmem_limit_bytes=56 * 1024 * 1024
        ),
    )(coarse_states[0], first_kernels, second_kernels, coarse_channel_gain)


def solution(mesh):
    depths, spaces = mesh.shape["depth"], mesh.shape["space"]
    placed = (
        P("depth", "space", None, None),
        P("depth", None, None, None),
        P("depth", None, None, None),
        P(),
    )
    return jax.shard_map(
        functools.partial(shards, depths, spaces),
        mesh=mesh,
        in_specs=placed,
        out_specs=(P("depth", "space", None, None), P("depth", "space", None, None)),
        check_vma=False,
    )
```

profile of v0, /device:TPU:29, one launch (start us, length us, event | category | flops | bytes accessed | tf_op | source)
XLA Modules:
  0.0 71.1 jit_solution(18215552756297227761)
XLA Ops:
  0.6 66.4 %shard_map.59 = (f32[4,8,128,128]{3,2,1,0:T(8,128)}, f32[1,8,128,128]{3,2,1,0:T(8,128)}) custom-call(f32[8,128,128]{2,1,0:T(8,128)} %bitcast.1, bf16[4,9,128,128]{3,2,1,0:T(8,128)(2,1)} %first_ref.1, bf16[4,9,128,128]{3,2,1,0:T(8,128)(2,1)} %second_ref.1, f32[8,128]{1,0:T(8,128)} %gain_ref.1), custom_call_target="tpu_custom_call" | custom-call | tf_op jit(solution)/shard_map/pallas_call | solution.py:319
  67.1 0.0 copy-start
  67.1 3.2 %copy.8 = f32[4,8,128,128]{3,2,1,0:T(8,128)} copy(f32[4,8,128,128]{3,2,1,0:T(8,128)} %get-tuple-element.4) | data formatting | bytes 4194304
  70.3 0.0 copy-done
  70.3 0.8 %copy.9 = f32[1,8,128,128]{3,2,1,0:T(8,128)} copy(f32[1,8,128,128]{3,2,1,0:T(8,128)S(1)} %copy-done) | data formatting | bytes 1048576
Async XLA Ops:
  67.1 3.2 %copy-start = (f32[1,8,128,128]{3,2,1,0:T(8,128)S(1)}, f32[1,8,128,128]{3,2,1,0:T(8,128)}, u32[]{:S(2)}) copy-start(f32[1,8,128,128]{3,2,1,0:T(8,128)} %get-tuple-element.5) | copy-start | bytes 1572868
where the time goes:
time: 71.3 us; the launch traced here: 71.1 us
  Pallas kernels  66.4 us (93%)
  local copies, waits for them, and re-layouts  3.99 us (6%)
    pallas_call x1, Pallas kernels, shards(): pl.pallas_call(functools.partial(cycle_kernel, depths, spaces), out_shape...  66.4 us
    unnamed x4, local copies, waits for them, and re-layouts  3.99 us

commit v1 on v0

--- a/solution.py
+++ b/solution.py
@@ -114,33 +114,40 @@
             device_id_type=MESH,
         )
 
-    def halo_start(slot):
-        @pl.when(s > 0)
+    def halo_start(slot, side):
+        @pl.when((side == 0) & (s > 0))
         def _():
             halo_up(slot).start()
 
-        @pl.when(s < spaces - 1)
+        @pl.when((side == 1) & (s < spaces - 1))
         def _():
             halo_down(slot).start()
 
-    def halo_wait(slot):
-        @pl.when(s < spaces - 1)
+    def halo_wait(slot, side):
+        @pl.when((side == 0) & (s > 0))
+        def _():
+            halo_down(slot).wait_recv()
+            halo_up(slot).wait_send()
+
+        @pl.when((side == 1) & (s < spaces - 1))
         def _():
             halo_up(slot).wait_recv()
             halo_down(slot).wait_send()
 
-        @pl.when(s > 0)
-        def _():
-            halo_down(slot).wait_recv()
-            halo_up(slot).wait_send()
-
-    def layer(index, slot, src, dst, keep):
-        def hidden_rows(starts):
+    last_side = s % 2
+
+    def layer(index, slot, src, dst, keep, inner_done, edge_done):
+        def hidden_rows(starts, side=None):
             out = conv_pairs(lambda r: xbuf[slot, r], starts, lambda k: first_ref[index, k])
             out = jnp.tanh(out).astype(BF16)
             for n, r in enumerate(starts):
-                hbuf[r] = out[n * cols : (n + 1) * cols, :chans]
-                hbuf[r + 1] = out[n * cols : (n + 1) * cols, chans:]
+                one = out[n * cols : (n + 1) * cols, :chans]
+                two = out[n * cols : (n + 1) * cols, chans:]
+                if side is not None:
+                    one = jnp.where((side == 0) & (s == 0), jnp.zeros_like(one), one)
+                    two = jnp.where((side == 1) & (s == spaces - 1), jnp.zeros_like(two), two)
+                hbuf[r] = one
+                hbuf[r + 1] = two
 
         def state_rows(starts):
             out = conv_pairs(lambda r: hbuf[r], starts, lambda k: second_ref[index, k])
@@ -153,22 +160,17 @@
 
         hidden_rows(range(2, rows, 2))
         state_rows(range(2, rows - 2, 2))
-        halo_wait(slot)
-        hidden_rows((0, rows))
-
-        @pl.when(s == 0)
-        def _():
-            hbuf[0] = jnp.zeros_like(hbuf[0])
-
-        @pl.when(s == spaces - 1)
-        def _():
-            hbuf[rows + 1] = jnp.zeros_like(hbuf[rows + 1])
-
-        state_rows((0, rows - 2))
-
-        @pl.when(keep)
-        def _():
-            halo_start(1 - slot)
+        inner_done()
+        for side in (1 - last_side, last_side):
+            halo_wait(slot, side)
+            hidden_rows((side * rows,), side)
+            state_rows((side * (rows - 2),))
+
+            @pl.when(keep)
+            def _():
+                halo_start(1 - slot, side)
+
+            edge_done(side)
 
     @pl.when(s == 0)
     def _():
@@ -182,66 +184,108 @@
 
     def begin(slot, source):
         xbuf[slot, pl.ds(2, rows)] = sbuf[source].astype(BF16)
-        halo_start(slot)
+        for side in range(2):
+            halo_start(slot, side)
 
     sbuf[layers] = start_ref[...]
     begin(0, layers)
 
+    def y_copy(first, count, k):
+        return pltpu.make_async_remote_copy(
+            src_ref=ybuf.at[pl.ds(first, count)],
+            dst_ref=cbuf.at[pl.ds(first, count)],
+            send_sem=y_send.at[k],
+            recv_sem=y_recv.at[k],
+            device_id=(d + 1, s),
+            device_id_type=MESH,
+        )
+
+    y_parts = ((2, rows - 4, 2), (0, 2, 0), (rows - 2, 2, 1))
+
+    def y_out(first, count, k, slot):
+        ybuf[pl.ds(first, count)] = xbuf[1 - slot, pl.ds(first + 2, count)]
+
+        @pl.when(d < depths - 1)
+        def _():
+            y_copy(first, count, k).start()
+
     def first_sweep(i, carry):
-        layer(i, i % 2, layers, layers, i < layers - 1)
+        slot = i % 2
+
+        def inner_done():
+            @pl.when(i == layers - 1)
+            def _():
+                y_out(2, rows - 4, 2, slot)
+
+        def edge_done(side):
+            @pl.when(i == layers - 1)
+            def _():
+                y_out(side * (rows - 2), 2, side, slot)
+
+        layer(i, slot, layers, layers, i < layers - 1, inner_done, edge_done)
         return carry
 
     lax.fori_loop(0, layers, first_sweep, 0)
 
-    y_copy = pltpu.make_async_remote_copy(
-        src_ref=ybuf,
-        dst_ref=cbuf,
-        send_sem=y_send,
-        recv_sem=y_recv,
-        device_id=(d + 1, s),
-        device_id_type=MESH,
-    )
-    ybuf[...] = sbuf[layers].astype(BF16)
-
-    @pl.when(d < depths - 1)
-    def _():
-        y_copy.start()
-
     @pl.when(d == 0)
     def _():
         sbuf[0] = start_ref[...]
 
     @pl.when(d > 0)
     def _():
-        y_copy.wait_recv()
-        sbuf[0] = cbuf[...].astype(F32)
+        for first, count, k in y_parts:
+            y_copy(first, count, k).wait_recv()
+            sbuf[0, pl.ds(first, count)] = cbuf[pl.ds(first, count)].astype(F32)
 
     begin(layers % 2, 0)
 
+    part = cols // 2
+    mine = odd * half
+    theirs = half - mine
+
+    def scan_copy(kind, r, h, src, dst, device):
+        return pltpu.make_async_remote_copy(
+            src_ref=src.at[r, pl.ds(h * part, part)],
+            dst_ref=dst.at[r, pl.ds(h * part, part)],
+            send_sem=scan_send.at[kind, r, h],
+            recv_sem=scan_recv.at[kind, r, h],
+            device_id=(device, s),
+            device_id_type=MESH,
+        )
+
+    def q_out(first, count):
+        for k in range(count):
+            r = first + k
+            qsend[r] = (sbuf[layers, theirs + r] - ybuf[theirs + r].astype(F32)).astype(BF16)
+            for h in range(2):
+                scan_copy(0, r, h, qsend, qrecv, partner).start()
+
     def second_sweep(i, carry):
-        layer(i, (layers + i) % 2, layers * ((i + layers - 1) // layers), layers, i < layers - 1)
+        def inner_done():
+            @pl.when(i == layers - 1)
+            def _():
+                q_out(2 * odd, half - 2)
+
+        def edge_done(side):
+            @pl.when((i == layers - 1) & (side == 1 - odd))
+            def _():
+                q_out((1 - odd) * (half - 2), 2)
+
+        layer(
+            i,
+            (layers + i) % 2,
+            layers * ((i + layers - 1) // layers),
+            layers,
+            i < layers - 1,
+            inner_done,
+            edge_done,
+        )
         return carry
 
     lax.fori_loop(0, layers, second_sweep, 0)
 
     relaxed_copy = pltpu.make_async_copy(sbuf.at[layers], relaxed_ref.at[0], relaxed_sem)
     relaxed_copy.start()
-
-    def scan_copy(kind, r, src, dst, device):
-        return pltpu.make_async_remote_copy(
-            src_ref=src.at[r],
-            dst_ref=dst.at[r],
-            send_sem=scan_send.at[kind, r],
-            recv_sem=scan_recv.at[kind, r],
-            device_id=(device, s),
-            device_id_type=MESH,
-        )
-
-    mine = odd * half
-    theirs = half - mine
-    for r in range(half):
-        qsend[r] = (sbuf[layers, theirs + r] - ybuf[theirs + r].astype(F32)).astype(BF16)
-        scan_copy(0, r, qsend, qrecv, partner).start()
 
     even = d - odd
     gain_odd = gain_ref[pl.ds((even + 1) % depths, 1), :]
@@ -251,31 +295,35 @@
     def _():
         trecv[...] = jnp.zeros_like(trecv)
 
-    for r in range(half):
-        own = sbuf[layers, mine + r] - ybuf[mine + r].astype(F32)
-        scan_copy(0, r, qsend, qrecv, partner).wait_recv()
-        other = qrecv[r].astype(F32)
+    order = [((k + (1 - odd) * 2) % half, h) for k in range(half) for h in range(2)]
+    for r, h in order:
+        piece = pl.ds(h * part, part)
+        own = sbuf[layers, mine + r, piece] - ybuf[mine + r, piece].astype(F32)
+        scan_copy(0, r, h, qsend, qrecv, partner).wait_recv()
+        other = qrecv[r, piece].astype(F32)
         q_even = jnp.where(odd == 0, own, other)
         q_odd = jnp.where(odd == 0, other, own)
 
         @pl.when(d > 1)
         def _():
-            scan_copy(1, r, tsend, trecv, d + 2).wait_recv()
-
-        e_even = trecv[r].astype(F32)
+            scan_copy(1, r, h, tsend, trecv, d + 2).wait_recv()
+
+        e_even = trecv[r, piece].astype(F32)
         e_odd = gain_odd * e_even + q_even
 
         @pl.when(d < depths - 2)
         def _():
-            tsend[r] = (gain_next * e_odd + q_odd).astype(BF16)
-            scan_copy(1, r, tsend, trecv, d + 2).start()
-
-        fsend[r] = jnp.where(odd == 0, e_odd, e_even).astype(BF16)
-        scan_copy(2, r, fsend, frecv, partner).start()
-        sbuf[0, mine + r] = sbuf[0, mine + r] + jnp.where(odd == 0, e_even, e_odd)
-
-    for r in range(half):
-        scan_copy(2, r, fsend, frecv, partner).wait_recv()
+            tsend[r, piece] = (gain_next * e_odd + q_odd).astype(BF16)
+            scan_copy(1, r, h, tsend, trecv, d + 2).start()
+
+        fsend[r, piece] = jnp.where(odd == 0, e_odd, e_even).astype(BF16)
+        scan_copy(2, r, h, fsend, frecv, partner).start()
+        sbuf[0, mine + r, piece] = sbuf[0, mine + r, piece] + jnp.where(odd == 0, e_even, e_odd)
+
+    for k in range(half):
+        r = (k + odd * 2) % half
+        for h in range(2):
+            scan_copy(2, r, h, fsend, frecv, partner).wait_recv()
         sbuf[0, theirs + r] = sbuf[0, theirs + r] + frecv[r].astype(F32)
 
     begin((2 * layers) % 2, 0)
@@ -286,7 +334,7 @@
     out_copy(0).start()
 
     def third_sweep(i, carry):
-        layer(i, i % 2, i, i + 1, i < layers - 2)
+        layer(i, i % 2, i, i + 1, i < layers - 2, lambda: None, lambda side: None)
         out_copy(i + 1).start()
         return carry
 
@@ -294,15 +342,17 @@
 
     @pl.when(d < depths - 1)
     def _():
-        y_copy.wait_send()
+        for first, count, k in y_parts:
+            y_copy(first, count, k).wait_send()
 
     for r in range(half):
-        scan_copy(0, r, qsend, qrecv, partner).wait_send()
-        scan_copy(2, r, fsend, frecv, partner).wait_send()
-
-        @pl.when(d < depths - 2)
-        def _():
-            scan_copy(1, r, tsend, trecv, d + 2).wait_send()
+        for h in range(2):
+            scan_copy(0, r, h, qsend, qrecv, partner).wait_send()
+            scan_copy(2, r, h, fsend, frecv, partner).wait_send()
+
+            @pl.when(d < depths - 2)
+            def _():
+                scan_copy(1, r, h, tsend, trecv, d + 2).wait_send()
 
     relaxed_copy.wait()
     for i in range(layers):
@@ -338,15 +388,15 @@
             part,
             pltpu.SemaphoreType.DMA((2, 2)),
             pltpu.SemaphoreType.DMA((2, 2)),
-            pltpu.SemaphoreType.DMA,
-            pltpu.SemaphoreType.DMA,
-            pltpu.SemaphoreType.DMA((3, half)),
-            pltpu.SemaphoreType.DMA((3, half)),
+            pltpu.SemaphoreType.DMA((3,)),
+            pltpu.SemaphoreType.DMA((3,)),
+            pltpu.SemaphoreType.DMA((3, half, 2)),
+            pltpu.SemaphoreType.DMA((3, half, 2)),
             pltpu.SemaphoreType.DMA((layers,)),
             pltpu.SemaphoreType.DMA,
         ],
         compiler_params=pltpu.CompilerParams(
-            collective_id=0, has_side_effects=True, vmem_limit_bytes=56 * 1024 * 1024
+            collective_id=0, has_side_effects=True, vmem_limit_bytes=24 * 1024 * 1024
         ),
     )(coarse_states[0], first_kernels, second_kernels, coarse_channel_gain)
 

time: 71.3 us -> 63.4 us (0.89)
  Pallas kernels: 66.4 us -> 56.1 us
  local copies, waits for them, and re-layouts: 3.99 us -> 6.38 us
    pallas_call x1, Pallas kernels: 66.4 us -> 56.1 us  [shards(): pl.pallas_call(functools.partial(cycle_kernel, depths, spaces), out_shape...]
    unnamed x4 -> x10, local copies, waits for them, and re-layouts: 3.99 us -> 6.38 us
where the time goes in v1:
time: 63.4 us; the launch traced here: 63.1 us
  Pallas kernels  56.1 us (88%)
  local copies, waits for them, and re-layouts  6.38 us (10%)
  between operations  0.65 us (1%)
    pallas_call x1, Pallas kernels, shards(): pl.pallas_call(functools.partial(cycle_kernel, depths, spaces), out_shape...  56.1 us
    unnamed x10, local copies, waits for them, and re-layouts  6.38 us

profile of v1, /device:TPU:29, one launch (start us, length us, event | category | flops | bytes accessed | tf_op | source)
XLA Modules:
  0.0 63.1 jit_solution(3820256960048235410)
XLA Ops:
  0.6 0.0 copy-start
  0.6 1.3 %copy-done = bf16[4,9,128,128]{3,2,1,0:T(8,128)(2,1)S(1)} copy-done((bf16[4,9,128,128]{3,2,1,0:T(8,128)(2,1)S(1)}, bf16[4,9,128,128]{3,2,1,0:T(8,128)(2,1)}, u32[]{:S(2)}) %copy-start) | copy-done | bytes 1179672
  1.9 0.0 copy-start.1
  1.9 1.3 %copy-done.1 = bf16[4,9,128,128]{3,2,1,0:T(8,128)(2,1)S(1)} copy-done((bf16[4,9,128,128]{3,2,1,0:T(8,128)(2,1)S(1)}, bf16[4,9,128,128]{3,2,1,0:T(8,128)(2,1)}, u32[]{:S(2)}) %copy-start.1) | copy-done | bytes 1179672
  3.2 0.0 copy-start.2
  3.2 1.0 %copy-done.2 = f32[1,8,128,128]{3,2,1,0:T(8,128)S(1)} copy-done((f32[1,8,128,128]{3,2,1,0:T(8,128)S(1)}, f32[1,8,128,128]{3,2,1,0:T(8,128)}, u32[]{:S(2)}) %copy-start.2) | copy-done | bytes 524312
  4.2 0.0 copy-start.3
  4.2 0.7 %copy-done.3 = f32[8,128]{1,0:T(8,128)S(1)} copy-done((f32[8,128]{1,0:T(8,128)S(1)}, f32[8,128]{1,0:T(8,128)}, u32[]{:S(2)}) %copy-start.3) | copy-done | bytes 4120
  4.9 56.1 %shard_map.59 = (f32[4,8,128,128]{3,2,1,0:T(8,128)S(1)}, f32[1,8,128,128]{3,2,1,0:T(8,128)S(1)}) custom-call(f32[8,128,128]{2,1,0:T(8,128)S(1)} %bitcast.1, bf16[4,9,128,128]{3,2,1,0:T(8,128)(2,1)S(1)} %copy-done, bf16[4,9,128,128]{3,2,1,0:T(8,128)(2,1)S(1)} %copy-done.1, f32[8,128]{1,0:T(8,128)S(1)} %copy-done.3), custom_call_target="tpu_custom_call" | custom-call | tf_op jit(solution)/shard_map/pallas_call | solution.py:369
  61.0 1.3 %copy.8 = f32[4,8,128,128]{3,2,1,0:T(8,128)} copy(f32[4,8,128,128]{3,2,1,0:T(8,128)S(1)} %get-tuple-element.4) | data formatting | bytes 4194304
  62.3 0.8 %copy.9 = f32[1,8,128,128]{3,2,1,0:T(8,128)} copy(f32[1,8,128,128]{3,2,1,0:T(8,128)S(1)} %get-tuple-element.5) | data formatting | bytes 1048576
Async XLA Ops:
  0.6 1.3 %copy-start = (bf16[4,9,128,128]{3,2,1,0:T(8,128)(2,1)S(1)}, bf16[4,9,128,128]{3,2,1,0:T(8,128)(2,1)}, u32[]{:S(2)}) copy-start(bf16[4,9,128,128]{3,2,1,0:T(8,128)(2,1)} %first_ref.1) | copy-start | bytes 3538948
  1.9 1.3 %copy-start.1 = (bf16[4,9,128,128]{3,2,1,0:T(8,128)(2,1)S(1)}, bf16[4,9,128,128]{3,2,1,0:T(8,128)(2,1)}, u32[]{:S(2)}) copy-start(bf16[4,9,128,128]{3,2,1,0:T(8,128)(2,1)} %second_ref.1) | copy-start | bytes 3538948
  3.2 1.0 %copy-start.2 = (f32[1,8,128,128]{3,2,1,0:T(8,128)S(1)}, f32[1,8,128,128]{3,2,1,0:T(8,128)}, u32[]{:S(2)}) copy-start(f32[1,8,128,128]{3,2,1,0:T(8,128)} %param.4) | copy-start | bytes 1572868
  4.2 0.7 %copy-start.3 = (f32[8,128]{1,0:T(8,128)S(1)}, f32[8,128]{1,0:T(8,128)}, u32[]{:S(2)}) copy-start(f32[8,128]{1,0:T(8,128)} %gain_ref.1) | copy-start | bytes 12292
